TPU v7x, 32 devices: a whole 2x2x4 slice. The times are simulated.
32 devices in a mesh: dp: 16 (over z, y, core), mp: 2 (over x).
Axes of the slice: x: 2, y: 2, z: 4, core: 2. Of those that a mesh axis runs over, the one named last changes fastest.
Arguments:
- inputs: bfloat16 [64, 320, 1024], P('dp', 'mp'), may hold values from -6 to 6
- teacher: bfloat16 [64, 320, 1024], P('dp', 'mp'), may hold values from -6 to 6
- keep_mask: int32 [64, 320], P('dp'), may hold values from 0 to 1, as said below
- gain_attn: bfloat16 [1024], P('dp'), may hold values from 0.099609375 to 1.8984375
- qkv_weight: bfloat16 [1024, 3, 1024], P('dp', None, 'mp'), may hold values from -0.25 to 0.25
- out_weight: bfloat16 [1024, 1024], P('dp', 'mp'), may hold values from -0.5 to 0.5
- gain_mlp: bfloat16 [1024], P('dp'), may hold values from 0.099609375 to 1.8984375
- up_weight: bfloat16 [1024, 4096], P('dp', 'mp'), may hold values from -0.1875 to 0.1875
- down_weight: bfloat16 [1024, 4096], P('dp', 'mp'), may hold values from -0.125 to 0.125
Outputs:
- output: bfloat16 [64, 320, 1024], P('dp', 'mp')
- loss: float32 [], replicated
- input_grad: float32 [64, 320, 1024], P('dp', 'mp')
- gain_attn_grad: float32 [1024], P('dp')
- qkv_grad: float32 [1024, 3, 1024], P('dp', None, 'mp')
- out_grad: float32 [1024, 1024], P('dp', 'mp')
- gain_mlp_grad: float32 [1024], P('dp')
- up_grad: float32 [1024, 4096], P('dp', 'mp')
- down_grad: float32 [1024, 4096], P('dp', 'mp')
Inputs may be any that keep to these rules, and one draw needn't show every extreme that they name: `keep_mask`: the first 64 positions of every image are 1; how many of its other positions an image keeps varies from image to image and from draw to draw.
All inputs are finite; a program needn't handle non-finite values.
Results may differ from a plain program's by a relative error of at most 0.009.
The roundings to bfloat16 on the way count: a program that leaves them out, or rounds other values in their place, can miss the bound.
Values may be sent and summed in bfloat16 or wider, within the bound.
A program may use at most 96 MiB of HBM per device.

v0:
```python
import jax
import jax.numpy as jnp
from jax import lax
from jax.sharding import PartitionSpec as P

HDIM = 64
MICRO = 2
norm_epsilon = 1e-06


def normalize(values):
    centre = values - jnp.mean(values, axis=-1, keepdims=True)
    spread = jnp.mean(centre * centre, axis=-1, keepdims=True)
    scaled = lax.rsqrt(spread + norm_epsilon)
    return (centre * scaled, scaled)


def norm_back(grad_out, unit_rows, scaled, gain_values):
    grad_scaled = grad_out * gain_values
    first = jnp.mean(grad_scaled, axis=-1, keepdims=True)
    second = jnp.mean(grad_scaled * unit_rows, axis=-1, keepdims=True)
    return scaled * (grad_scaled - first - unit_rows * second)


def exact_gelu(values):
    return jax.nn.gelu(values, approximate=False)


def full_rows(piece):
    return lax.all_gather(piece, "mp", axis=1, tiled=True)


def row_sums(partial_rows):
    return lax.psum_scatter(partial_rows, "mp", scatter_dimension=1, tiled=True)


def full_grads(piece):
    return lax.all_gather(piece, "mp", axis=1, tiled=True)


def sum_grads(partial_rows):
    return lax.psum_scatter(partial_rows, "mp", scatter_dimension=1, tiled=True)


def split_heads(projected):
    image_count, seq_length = (projected.shape[0], projected.shape[1])
    head_count = projected.shape[3] // HDIM
    queries = projected[:, :, 0].reshape(image_count, seq_length, head_count, HDIM)
    key_rows = projected[:, :, 1].reshape(image_count, seq_length, head_count, HDIM)
    value_rows = projected[:, :, 2].reshape(image_count, seq_length, head_count, HDIM)
    return (queries, key_rows, value_rows)


def masked_scores(queries, key_rows, allowed):
    scores = jnp.einsum(
        "bqhe,bkhe->bhqk", queries, key_rows, preferred_element_type=jnp.float32
    ) * HDIM ** (-0.5)
    return jnp.where(allowed, scores, -1e30)


def attend(projected, allowed):
    queries, key_rows, value_rows = split_heads(projected)
    scores = masked_scores(queries, key_rows, allowed)
    maximum = jnp.max(scores, axis=-1, keepdims=True)
    raised = jnp.exp(scores - maximum)
    normaliser = jnp.sum(raised, axis=-1, keepdims=True)
    weights_soft = (raised / normaliser).astype(jnp.bfloat16)
    log_total = maximum + jnp.log(normaliser)
    mixture = jnp.einsum(
        "bhqk,bkhe->bqhe", weights_soft, value_rows, preferred_element_type=jnp.float32
    )
    shaped = mixture.reshape(projected.shape[0], projected.shape[1], projected.shape[3])
    return (shaped.astype(jnp.bfloat16), log_total)


def attend_back(projected, allowed, log_total, grad_heads):
    queries, key_rows, value_rows = split_heads(projected)
    scores = masked_scores(queries, key_rows, allowed)
    weights_soft = jnp.exp(scores - log_total)
    grad_mix = grad_heads.reshape(queries.shape)
    grad_weights = jnp.einsum(
        "bqhe,bkhe->bhqk", grad_mix, value_rows, preferred_element_type=jnp.float32
    )
    inner = jnp.sum(grad_weights * weights_soft, axis=-1, keepdims=True)
    grad_scores = (weights_soft * (grad_weights - inner)).astype(jnp.bfloat16)
    grad_query = jnp.einsum(
        "bhqk,bkhe->bqhe", grad_scores, key_rows, preferred_element_type=jnp.float32
    ) * HDIM ** (-0.5)
    grad_key = jnp.einsum(
        "bhqk,bqhe->bkhe", grad_scores, queries, preferred_element_type=jnp.float32
    ) * HDIM ** (-0.5)
    grad_value = jnp.einsum(
        "bhqk,bqhe->bkhe",
        weights_soft.astype(jnp.bfloat16),
        grad_mix,
        preferred_element_type=jnp.float32,
    )
    stacked = jnp.stack(
        [
            grad_query.astype(jnp.bfloat16),
            grad_key.astype(jnp.bfloat16),
            grad_value.astype(jnp.bfloat16),
        ],
        axis=2,
    )
    return stacked.reshape(projected.shape)


def per_device(
    inputs, teacher, keep_mask, gain_attn, qkv_weight, out_weight, gain_mlp, up_weight, down_weight
):
    owned = (gain_attn, gain_mlp, qkv_weight, out_weight, up_weight, down_weight)
    half_len = inputs.shape[1]
    offset = lax.axis_index("mp") * half_len
    keep_local = lax.dynamic_slice_in_dim(keep_mask, offset, half_len, 1)
    valid_total = lax.psum(jnp.sum(keep_local).astype(jnp.float32), ("dp", "mp"))
    token_total = inputs.shape[0] * lax.axis_size("dp") * half_len * lax.axis_size("mp")
    loss_factor = 2.0 * token_total / valid_total
    per_micro = inputs.shape[0] // MICRO
    summed = tuple(
        (
            jnp.zeros((piece.shape[0] * lax.axis_size("dp"),) + piece.shape[1:], jnp.float32)
            for piece in owned
        )
    )
    outputs = []
    input_grads = []
    loss_local = jnp.zeros((), jnp.float32)
    for micro_step in range(MICRO):
        first_image = micro_step * per_micro
        field_in = inputs[first_image : first_image + per_micro].astype(jnp.float32)
        target = teacher[first_image : first_image + per_micro].astype(jnp.float32)
        keep_rows = keep_local[first_image : first_image + per_micro].astype(jnp.float32)[
            :, :, None
        ]
        allowed = (keep_mask[first_image : first_image + per_micro] > 0)[:, None, None, :]
        forward_set = (
            lax.all_gather(gain_attn, "dp", axis=0, tiled=True),
            lax.all_gather(gain_mlp, "dp", axis=0, tiled=True),
            lax.all_gather(qkv_weight, "dp", axis=0, tiled=True),
            lax.all_gather(out_weight, "dp", axis=0, tiled=True),
            lax.all_gather(up_weight, "dp", axis=0, tiled=True),
            lax.all_gather(down_weight, "dp", axis=0, tiled=True),
        )
        gain_one = forward_set[0].astype(jnp.float32)
        gain_two = forward_set[1].astype(jnp.float32)
        w_qkv, w_out, w_up, w_down = (
            forward_set[2],
            forward_set[3],
            forward_set[4],
            forward_set[5],
        )
        unit_one, scaled_one = normalize(field_in)
        normed_full = full_rows((unit_one * gain_one).astype(jnp.bfloat16))
        projected = jnp.einsum(
            "bsd,dcf->bscf", normed_full, w_qkv, preferred_element_type=jnp.float32
        ).astype(jnp.bfloat16)
        heads_out, log_total = attend(projected, allowed)
        attended = row_sums(
            jnp.einsum("bsf,df->bsd", heads_out, w_out, preferred_element_type=jnp.float32)
        )
        middle = field_in + attended
        unit_two, scaled_two = normalize(middle)
        normed_wide = full_rows((unit_two * gain_two).astype(jnp.bfloat16))
        hidden_in = jnp.einsum("bsd,df->bsf", normed_wide, w_up, preferred_element_type=jnp.float32)
        activated, gelu_back = jax.vjp(exact_gelu, hidden_in)
        hidden = activated.astype(jnp.bfloat16)
        branch = row_sums(
            jnp.einsum("bsf,df->bsd", hidden, w_down, preferred_element_type=jnp.float32)
        )
        result = middle + branch
        outputs.append((result * keep_rows).astype(jnp.bfloat16))
        error = result - target
        loss_local = loss_local + jnp.sum(
            keep_rows * jnp.mean(error * error, axis=-1, keepdims=True)
        )
        grad_result = loss_factor * keep_rows * error
        backward_set = (
            lax.all_gather(gain_attn, "dp", axis=0, tiled=True),
            lax.all_gather(gain_mlp, "dp", axis=0, tiled=True),
            lax.all_gather(qkv_weight, "dp", axis=0, tiled=True),
            lax.all_gather(out_weight, "dp", axis=0, tiled=True),
            lax.all_gather(up_weight, "dp", axis=0, tiled=True),
            lax.all_gather(down_weight, "dp", axis=0, tiled=True),
        )
        w_qkv, w_out, w_up, w_down = (
            backward_set[2],
            backward_set[3],
            backward_set[4],
            backward_set[5],
        )
        grad_branch = full_grads(grad_result.astype(jnp.bfloat16))
        grad_hidden = jnp.einsum(
            "bsd,df->bsf", grad_branch, w_down, preferred_element_type=jnp.float32
        )
        down_part = jnp.einsum(
            "bsd,bsf->df", grad_branch, hidden, preferred_element_type=jnp.float32
        )
        grad_pre = gelu_back(grad_hidden)[0].astype(jnp.bfloat16)
        up_part = jnp.einsum(
            "bsd,bsf->df", normed_wide, grad_pre, preferred_element_type=jnp.float32
        )
        grad_normed_two = sum_grads(
            jnp.einsum("bsf,df->bsd", grad_pre, w_up, preferred_element_type=jnp.float32)
        )
        gain_mlp_part = jnp.sum(grad_normed_two * unit_two, axis=(0, 1))
        grad_middle = grad_result + norm_back(grad_normed_two, unit_two, scaled_two, gain_two)
        grad_attended = full_grads(grad_middle.astype(jnp.bfloat16))
        grad_heads = jnp.einsum(
            "bsd,df->bsf", grad_attended, w_out, preferred_element_type=jnp.float32
        ).astype(jnp.bfloat16)
        out_part = jnp.einsum(
            "bsd,bsf->df", grad_attended, heads_out, preferred_element_type=jnp.float32
        )
        grad_projected = attend_back(projected, allowed, log_total, grad_heads)
        qkv_part = jnp.einsum(
            "bsd,bscf->dcf", normed_full, grad_projected, preferred_element_type=jnp.float32
        )
        grad_normed_one = sum_grads(
            jnp.einsum("bscf,dcf->bsd", grad_projected, w_qkv, preferred_element_type=jnp.float32)
        )
        gain_attn_part = jnp.sum(grad_normed_one * unit_one, axis=(0, 1))
        input_grads.append(grad_middle + norm_back(grad_normed_one, unit_one, scaled_one, gain_one))
        fresh = (gain_attn_part, gain_mlp_part, qkv_part, out_part, up_part, down_part)
        summed = tuple((current + added for current, added in zip(summed, fresh)))
    summed = (
        lax.psum_scatter(summed[0], "dp", scatter_dimension=0, tiled=True),
        lax.psum_scatter(summed[1], "dp", scatter_dimension=0, tiled=True),
        lax.psum_scatter(summed[2], "dp", scatter_dimension=0, tiled=True),
        lax.psum_scatter(summed[3], "dp", scatter_dimension=0, tiled=True),
        lax.psum_scatter(summed[4], "dp", scatter_dimension=0, tiled=True),
        lax.psum_scatter(summed[5], "dp", scatter_dimension=0, tiled=True),
    )
    gain_sums = lax.psum((summed[0], summed[1]), "mp")
    loss = lax.psum(loss_local, ("dp", "mp")) / valid_total
    output = jnp.concatenate(outputs, axis=0)
    input_grad = jnp.concatenate(input_grads, axis=0)
    return (
        output,
        loss,
        input_grad,
        gain_sums[0],
        summed[2],
        summed[3],
        gain_sums[1],
        summed[4],
        summed[5],
    )


def solution(mesh):
    in_specs = (
        P("dp", "mp", None),
        P("dp", "mp", None),
        P("dp", None),
        P("dp"),
        P("dp", None, "mp"),
        P("dp", "mp"),
        P("dp"),
        P("dp", "mp"),
        P("dp", "mp"),
    )
    out_specs = (
        P("dp", "mp", None),
        P(),
        P("dp", "mp", None),
        P("dp"),
        P("dp", None, "mp"),
        P("dp", "mp"),
        P("dp"),
        P("dp", "mp"),
        P("dp", "mp"),
    )
    return jax.shard_map(
        per_device, mesh=mesh, in_specs=in_specs, out_specs=out_specs, check_vma=False
    )
```

profile of v0, /device:TPU:0, one launch (start us, length us, event | category | flops | bytes accessed | tf_op | source)
XLA Modules:
  0.0 1162.6 jit_solution(9195493048433533163)
XLA Ops:
  10.9 34.9 %all-reduce.6 = (bf16[1024]{0:T(1024)(128)(2,1)S(1)}, bf16[1024]{0:T(1024)(128)(2,1)S(1)}) all-reduce(bf16[1024]{0:T(1024)(128)(2,1)S(1)} %dynamic-update-slice, bf16[1024]{0:T(1024)(128)(2,1)S(1)} %dynamic-update-slice.1), channel_id=1, replica_groups=mesh['dp'=16,'mp'=2] {'dp'}, use_global_device_ids=true, to_apply=%add | all-reduce | flops 2048 | bytes 8192
  49.3 2.8 fusion.93
  54.3 19.5 %all-gather.13.cloned.1.call-done = bf16[2,320,1024]{2,1,0:T(8,128)(2,1)} async-done(((bf16[2,160,1024]{2,1,0:T(8,128)(2,1)}), bf16[2,320,1024]{2,1,0:T(8,128)(2,1)}) %all-gather.13.cloned.1.call-update) | async-done | bytes 1310736 | tf_op jit(solution)/shard_map/all_gather | solution.py:30
  73.8 47.4 %all-gather.15.cloned.1.call-done = bf16[1024,3,512]{2,0,1:T(8,128)(2,1)} async-done(((bf16[64,3,512]{2,0,1:T(8,128)(2,1)}), bf16[1024,3,512]{2,0,1:T(8,128)(2,1)}) %all-gather.15.cloned.1.call-update) | async-done | bytes 3145744 | tf_op jit(solution)/shard_map/all_gather | solution.py:140
  121.2 4.5 fusion.54
  134.9 25.3 %all-gather.17.cloned.1.call-done = bf16[1024,512]{1,0:T(8,128)(2,1)} async-done(((bf16[64,512]{1,0:T(8,128)(2,1)}), bf16[1024,512]{1,0:T(8,128)(2,1)}) %all-gather.17.cloned.1.call-update) | async-done | bytes 1048592 | tf_op jit(solution)/shard_map/all_gather | solution.py:141
  160.2 3.9 fusion.113
  164.7 20.1 %all-gather.25.cloned.1.call-done = bf16[2,320,1024]{2,1,0:T(8,128)(2,1)} async-done(((bf16[2,160,1024]{2,1,0:T(8,128)(2,1)}), bf16[2,320,1024]{2,1,0:T(8,128)(2,1)}) %all-gather.25.cloned.1.call-update) | async-done | bytes 1310736 | tf_op jit(solution)/shard_map/all_gather | solution.py:30
  184.8 4.5 fusion.57
  198.5 2.7 fusion.111
  202.1 23.0 %reduce-scatter.13.cloned.1.call-done = f32[2,160,1024]{2,1,0:T(8,128)} async-done(((f32[2,320,1024]{2,1,0:T(8,128)}), f32[2,160,1024]{2,1,0:T(8,128)}) %reduce-scatter.13.cloned.1.call-update) | async-done | bytes 1310736 | tf_op jit(solution)/shard_map/reduce_scatter | solution.py:34
  225.1 39.8 %reduce-scatter.17.cloned.1.call-done = f32[2,160,1024]{2,1,0:T(8,128)} async-done(((f32[2,320,1024]{2,1,0:T(8,128)}), f32[2,160,1024]{2,1,0:T(8,128)}) %reduce-scatter.17.cloned.1.call-update) | async-done | bytes 1310736 | tf_op jit(solution)/shard_map/reduce_scatter | solution.py:34
  264.9 2.5 fusion.130
  270.9 46.7 %all-gather.21.cloned.1.call-done = bf16[1024,2048]{1,0:T(8,128)(2,1)} async-done(((bf16[64,2048]{1,0:T(8,128)(2,1)}), bf16[1024,2048]{1,0:T(8,128)(2,1)}) %all-gather.21.cloned.1.call-update) | async-done | bytes 4194320 | tf_op jit(solution)/shard_map/all_gather | solution.py:142
  317.6 24.9 %all-gather.19.cloned.1.call-done = bf16[2,320,1024]{2,1,0:T(8,128)(2,1)} async-done(((bf16[2,160,1024]{2,1,0:T(8,128)(2,1)}), bf16[2,320,1024]{2,1,0:T(8,128)(2,1)}) %all-gather.19.cloned.1.call-update) | async-done | bytes 1310736 | tf_op jit(solution)/shard_map/all_gather | solution.py:30
  342.5 6.9 fusion.107
  351.7 12.9 %multiply_convert_fusion.3 = (bf16[2,320,2048]{2,1,0:T(8,128)(2,1)}, f32[2,320,2048]{2,1,0:T(8,128)}) fusion(f32[2,320,2048]{2,1,0:T(8,128)S(1)} %get-tuple-element.87, u8[320,2048]{1,0:T(8,128)(4,1)S(1)} %get-tuple-element.10, u8[320,2048]{1,0:T(8,128)(4,1)S(1)} %get-tuple-element.9), kind=kLoop, calls=%fused_computation.47 | loop fusion | flops 91750400 | bytes 14417920 | tf_op jit(solution)/shard_map/convert_element_type | solution.py:167
  364.6 30.7 %all-gather.23.cloned.1.call-done = bf16[1024,2048]{1,0:T(8,128)(2,1)} async-done(((bf16[64,2048]{1,0:T(8,128)(2,1)}), bf16[1024,2048]{1,0:T(8,128)(2,1)}) %all-gather.23.cloned.1.call-update) | async-done | bytes 4194320 | tf_op jit(solution)/shard_map/all_gather | solution.py:143
  395.3 7.4 fusion.22
  402.9 16.5 %all-gather.27.cloned.1.call-done = bf16[2,320,1024]{2,1,0:T(8,128)(2,1)} async-done(((bf16[2,160,1024]{2,1,0:T(8,128)(2,1)}), bf16[2,320,1024]{2,1,0:T(8,128)(2,1)}) %all-gather.27.cloned.1.call-update) | async-done | bytes 1310736 | tf_op jit(solution)/shard_map/all_gather | solution.py:30
  419.5 6.9 fusion.108
  426.4 12.8 %multiply_convert_fusion.2 = (bf16[2,320,2048]{2,1,0:T(8,128)(2,1)S(1)}, f32[2,320,2048]{2,1,0:T(8,128)}) fusion(f32[2,320,2048]{2,1,0:T(8,128)S(1)} %get-tuple-element.86, u8[320,2048]{1,0:T(8,128)(4,1)S(1)} %get-tuple-element.12, u8[320,2048]{1,0:T(8,128)(4,1)S(1)} %get-tuple-element.11), kind=kLoop, calls=%fused_computation.34 | loop fusion | flops 91750400 | bytes 14417920 | tf_op jit(solution)/shard_map/convert_element_type | solution.py:167
  440.7 4.4 fusion.20
  446.6 39.7 %psum.29 = f32[]{:T(128)} all-reduce(f32[]{:T(128)S(6)} %convert_element_type.181), channel_id=1, replica_groups=mesh['dp'=16,'mp'=2] {'dp','mp'}, use_global_device_ids=true, to_apply=%region_22.23 | all-reduce | flops 1 | bytes 8 | tf_op jit(solution)/shard_map/psum | solution.py:116
  487.1 13.4 %reduce-scatter.19.cloned.1.call-done = f32[2,160,1024]{2,1,0:T(8,128)} async-done(((f32[2,320,1024]{2,1,0:T(8,128)}), f32[2,160,1024]{2,1,0:T(8,128)}) %reduce-scatter.19.cloned.1.call-update) | async-done | bytes 1310736 | tf_op jit(solution)/shard_map/reduce_scatter | solution.py:34
  500.4 3.6 multiply_convert_fusion.13
  505.1 23.4 %all-gather.29.cloned.1.call-done = bf16[2,320,1024]{2,1,0:T(8,128)(2,1)} async-done(((bf16[2,160,1024]{2,1,0:T(8,128)(2,1)}), bf16[2,320,1024]{2,1,0:T(8,128)(2,1)}) %all-gather.29.cloned.1.call-update) | async-done | bytes 1310736 | tf_op jit(solution)/shard_map/all_gather | solution.py:38
  528.5 10.0 add_convert_fusion.1
  540.0 4.4 fusion.26
  544.5 9.7 all-gather.33.cloned.1.call-done
  554.2 10.0 add_convert_fusion
  565.7 4.4 fusion.24
  570.4 23.5 %reduce-scatter.21.cloned.1.call-done = f32[2,160,1024]{2,1,0:T(8,128)} async-done(((f32[2,320,1024]{2,1,0:T(8,128)}), f32[2,160,1024]{2,1,0:T(8,128)}) %reduce-scatter.21.cloned.1.call-update) | async-done | bytes 1310736 | tf_op jit(solution)/shard_map/reduce_scatter | solution.py:42
  593.9 39.8 %reduce-scatter.25.cloned.1.call-done = f32[2,160,1024]{2,1,0:T(8,128)} async-done(((f32[2,320,1024]{2,1,0:T(8,128)}), f32[2,160,1024]{2,1,0:T(8,128)}) %reduce-scatter.25.cloned.1.call-update) | async-done | bytes 1310736 | tf_op jit(solution)/shard_map/reduce_scatter | solution.py:42
  633.7 4.4 multiply_reduce_fusion.2
  640.6 4.2 fusion.127
  644.9 20.0 %all-gather.35.cloned.1.call-done = bf16[2,320,1024]{2,1,0:T(8,128)(2,1)} async-done(((bf16[2,160,1024]{2,1,0:T(8,128)(2,1)}), bf16[2,320,1024]{2,1,0:T(8,128)(2,1)}) %all-gather.35.cloned.1.call-update) | async-done | bytes 1310736 | tf_op jit(solution)/shard_map/all_gather | solution.py:38
  664.9 3.0 convolution_convert_fusion
  670.1 7.2 multiply_reduce_fusion
  677.3 3.7 multiply_convert_fusion
  681.0 2.9 fusion.83
  686.2 3.8 multiply_convert_fusion.5
  692.2 3.4 multiply_convert_fusion.4
  696.0 6.1 fusion.63
  704.9 5.4 fusion.80
  711.4 5.2 multiply_reduce_fusion.1
  716.7 4.7 multiply_convert_fusion.1
  725.2 3.5 multiply_convert_fusion.6
  729.0 6.3 fusion.60
  735.4 2.5 fusion.136
  740.8 5.8 fusion.137
  746.6 6.1 bitcast_add_fusion.1
  754.4 5.0 fusion.138
  759.4 6.0 bitcast_add_fusion
  766.7 4.2 fusion.102
  771.0 4.8 bitcast_add_fusion.2
  779.5 39.3 %psum.28 = f32[]{:T(128)} all-reduce(f32[]{:T(128)S(6)} %add.141), channel_id=1, replica_groups=mesh['dp'=16,'mp'=2] {'dp','mp'}, use_global_device_ids=true, to_apply=%region_20.21 | all-reduce | flops 1 | bytes 8 | tf_op jit(solution)/shard_map/psum | solution.py:235
  822.5 2.9 fusion.98
  825.4 32.9 %all-reduce.4 = (f32[1024]{0:T(1024)S(1)}, f32[1024]{0:T(1024)S(1)}) all-reduce(f32[1024]{0:T(1024)S(1)} %add.148, f32[1024]{0:T(1024)S(1)} %add.151), channel_id=10, replica_groups=mesh['dp'=16,'mp'=2] {'dp'}, use_global_device_ids=true, to_apply=%region_39.40.clone | all-reduce | flops 2048 | bytes 16384
  858.4 5.4 all-reduce.5
  863.9 3.0 fusion.97
  868.5 86.4 %reduce-scatter.33.cloned.1.call-done = f32[64,2048]{1,0:T(8,128)} async-done(((f32[1024,2048]{1,0:T(8,128)}), f32[64,2048]{1,0:T(8,128)}) %reduce-scatter.33.cloned.1.call-update) | async-done | bytes 524304 | tf_op jit(solution)/shard_map/reduce_scatter | solution.py:231
  954.9 109.6 %reduce-scatter.35.cloned.1.call-done = f32[64,2048]{1,0:T(8,128)} async-done(((f32[1024,2048]{1,0:T(8,128)}), f32[64,2048]{1,0:T(8,128)}) %reduce-scatter.35.cloned.1.call-update) | async-done | bytes 524304 | tf_op jit(solution)/shard_map/reduce_scatter | solution.py:232
  1064.5 89.9 %reduce-scatter.29.cloned.1.call-done = f32[64,3,512]{2,0,1:T(8,128)} async-done(((f32[1024,3,512]{2,0,1:T(8,128)}), f32[64,3,512]{2,0,1:T(8,128)}) %reduce-scatter.29.cloned.1.call-update) | async-done | bytes 393232 | tf_op jit(solution)/shard_map/reduce_scatter | solution.py:229
  (252 shorter events, 70.2 us)
Async XLA Ops:
  7.2 47.1 %copy-start.47 = (s32[4,320]{1,0:T(4,128)S(1)}, s32[4,320]{1,0:T(4,128)}, u32[]{:S(2)}) copy-start(s32[4,320]{1,0:T(4,128)} %param.11) | copy-start | bytes 15364
  7.2 66.6 %all-gather.13.cloned.1.call-start = ((), (), s32[]{:S(2)}) async-start(), calls=%async_computation.12 | async-start | bytes 1966080 | tf_op jit(solution)/shard_map/all_gather | solution.py:30
  47.4 4.7 copy-start.43
  47.4 4.7 copy-start.45
  52.1 69.1 %all-gather.15.cloned.1.call-start = ((), (), s32[]{:S(2)}) async-start(), calls=%async_computation.13 | async-start | bytes 3342336 | tf_op jit(solution)/shard_map/all_gather | solution.py:140
  52.9 107.3 %all-gather.17.cloned.1.call-start = ((), (), s32[]{:S(2)}) async-start(), calls=%async_computation.14 | async-start | bytes 1114112 | tf_op jit(solution)/shard_map/all_gather | solution.py:141
  53.6 131.2 %all-gather.25.cloned.1.call-start = ((), (), s32[]{:S(2)}) async-start(), calls=%async_computation.20 | async-start | bytes 1966080 | tf_op jit(solution)/shard_map/all_gather | solution.py:30
  54.2 170.9 %reduce-scatter.13.cloned.1.call-start = ((), (), s32[]{:S(2)}) async-start(), calls=%async_computation.15 | async-start | bytes 3932160 | tf_op jit(solution)/shard_map/reduce_scatter | solution.py:34
  127.1 4.1 copy-start.18
  134.9 54.4 %copy-start.30 = (bf16[2,8,64,320]{3,2,1,0:T(8,128)(2,1)}, bf16[2,8,64,320]{3,2,1,0:T(8,128)(2,1)S(1)}, u32[]{:S(2)}) copy-start(bf16[2,8,64,320]{3,2,1,0:T(8,128)(2,1)S(1)} %fusion.79) | copy-start | bytes 1966084
  164.1 100.8 %reduce-scatter.17.cloned.1.call-start = ((), (), s32[]{:S(2)}) async-start(), calls=%async_computation.21 | async-start | bytes 3932160 | tf_op jit(solution)/shard_map/reduce_scatter | solution.py:34
  198.5 26.5 %copy-start.23 = (bf16[2,8,64,320]{3,2,1,0:T(8,128)(2,1)}, bf16[2,8,64,320]{3,2,1,0:T(8,128)(2,1)S(1)}, u32[]{:S(2)}) copy-start(bf16[2,8,64,320]{3,2,1,0:T(8,128)(2,1)S(1)} %fusion.78) | copy-start | bytes 1966084
  201.2 116.4 %all-gather.21.cloned.1.call-start = ((), (), s32[]{:S(2)}) async-start(), calls=%async_computation.17 | async-start | bytes 4456448 | tf_op jit(solution)/shard_map/all_gather | solution.py:142
  202.0 140.5 %all-gather.19.cloned.1.call-start = ((), (), s32[]{:S(2)}) async-start(), calls=%async_computation.16 | async-start | bytes 1966080 | tf_op jit(solution)/shard_map/all_gather | solution.py:30
  269.4 125.9 %all-gather.23.cloned.1.call-start = ((), (), s32[]{:S(2)}) async-start(), calls=%async_computation.18 | async-start | bytes 4456448 | tf_op jit(solution)/shard_map/all_gather | solution.py:143
  270.1 149.3 %all-gather.27.cloned.1.call-start = ((), (), s32[]{:S(2)}) async-start(), calls=%async_computation.22 | async-start | bytes 1966080 | tf_op jit(solution)/shard_map/all_gather | solution.py:30
  270.7 216.3 %reduce-scatter.15.cloned.1.call-start = ((), (), s32[]{:S(2)}) async-start(), calls=%async_computation.19 | async-start | bytes 3932160 | tf_op jit(solution)/shard_map/reduce_scatter | solution.py:34
  402.7 97.8 %reduce-scatter.19.cloned.1.call-start = ((), (), s32[]{:S(2)}) async-start(), calls=%async_computation.23 | async-start | bytes 3932160 | tf_op jit(solution)/shard_map/reduce_scatter | solution.py:34
  426.4 12.8 %copy-start.13 = (f32[2,320,2048]{2,1,0:T(8,128)}, f32[2,320,2048]{2,1,0:T(8,128)S(1)}, u32[]{:S(2)}) copy-start(f32[2,320,2048]{2,1,0:T(8,128)S(1)} %get-tuple-element.86) | copy-start | bytes 15728644
  426.4 14.3 %copy-start.57 = (bf16[1024,2048]{1,0:T(8,128)(2,1)S(1)}, bf16[1024,2048]{1,0:T(8,128)(2,1)}, u32[]{:S(2)}) copy-start(bf16[1024,2048]{1,0:T(8,128)(2,1)} %all-gather.23.cloned.1.call-done) | copy-start | bytes 12582916
  445.1 83.4 %all-gather.29.cloned.1.call-start = ((), (), s32[]{:S(2)}) async-start(), calls=%async_computation.24 | async-start | bytes 1966080 | tf_op jit(solution)/shard_map/all_gather | solution.py:38
  504.1 50.1 %all-gather.33.cloned.1.call-start = ((), (), s32[]{:S(2)}) async-start(), calls=%async_computation.28 | async-start | bytes 1966080 | tf_op jit(solution)/shard_map/all_gather | solution.py:38
  504.7 89.2 %reduce-scatter.21.cloned.1.call-start = ((), (), s32[]{:S(2)}) async-start(), calls=%async_computation.25 | async-start | bytes 3932160 | tf_op jit(solution)/shard_map/reduce_scatter | solution.py:42
  528.5 11.5 copy-start.55
  544.4 89.3 %reduce-scatter.25.cloned.1.call-start = ((), (), s32[]{:S(2)}) async-start(), calls=%async_computation.29 | async-start | bytes 3932160 | tf_op jit(solution)/shard_map/reduce_scatter | solution.py:42
  554.2 11.5 copy-start.56
  570.1 94.8 %all-gather.35.cloned.1.call-start = ((), (), s32[]{:S(2)}) async-start(), calls=%async_computation.30 | async-start | bytes 1966080 | tf_op jit(solution)/shard_map/all_gather | solution.py:38
  633.7 4.4 copy-start.4
  633.7 4.4 copy-start.5
  633.7 4.4 copy-start.14
  640.5 61.9 %all-gather.31.cloned.1.call-start = ((), (), s32[]{:S(2)}) async-start(), calls=%async_computation.26 | async-start | bytes 1966080 | tf_op jit(solution)/shard_map/all_gather | solution.py:38
  640.6 24.3 %copy-start.17 = (bf16[1024,512]{1,0:T(8,128)(2,1)S(1)}, bf16[1024,512]{1,0:T(8,128)(2,1)}, u32[]{:S(2)}) copy-start(bf16[1024,512]{1,0:T(8,128)(2,1)} %all-gather.17.cloned.1.call-done) | copy-start | bytes 3145732
  644.8 25.3 %copy-start.21 = (bf16[2,320,1,512]{1,3,0,2:T(8,128)(2,1)S(1)}, bf16[2,320,1,512]{1,3,0,2:T(8,128)(2,1)}, u32[]{:S(2)}) copy-start(bf16[2,320,1,512]{1,3,0,2:T(8,128)(2,1)} %copy-done.20) | copy-start | bytes 1966084
  644.8 177.6 %reduce-scatter.27.cloned.1.call-start = ((), (), s32[]{:S(2)}) async-start(), calls=%async_computation.31 | async-start | bytes 3932160 | tf_op jit(solution)/shard_map/reduce_scatter | solution.py:42
  670.1 7.2 slice-start
  670.1 7.2 slice-start.1
  681.0 5.1 copy-start.11
  695.9 6.4 copy-start.38
  696.0 6.4 copy-start.40
  702.1 120.4 %reduce-scatter.23.cloned.1.call-start = ((), (), s32[]{:S(2)}) async-start(), calls=%async_computation.27 | async-start | bytes 3932160 | tf_op jit(solution)/shard_map/reduce_scatter | solution.py:42
  704.9 6.5 copy-start.19
  716.6 6.6 copy-start.9
  729.0 6.3 copy-start.36
  729.0 6.4 copy-start.31
  735.3 133.2 %reduce-scatter.31.cloned.1.call-start = ((), (), s32[]{:S(2)}) async-start(), calls=%async_computation.33 | async-start | bytes 2228224 | tf_op jit(solution)/shard_map/reduce_scatter | solution.py:230
  740.3 6.3 copy-start.59
  740.3 214.6 %reduce-scatter.33.cloned.1.call-start = ((), (), s32[]{:S(2)}) async-start(), calls=%async_computation.34 | async-start | bytes 8912896 | tf_op jit(solution)/shard_map/reduce_scatter | solution.py:231
  740.8 5.8 copy-start.62
  752.7 311.8 %reduce-scatter.35.cloned.1.call-start = ((), (), s32[]{:S(2)}) async-start(), calls=%async_computation.35 | async-start | bytes 8912896 | tf_op jit(solution)/shard_map/reduce_scatter | solution.py:232
  754.4 5.0 copy-start.27
  754.4 5.0 copy-start.60
  765.4 5.5 copy-start.32
  765.4 5.5 copy-start.33
  765.4 389.0 %reduce-scatter.29.cloned.1.call-start = ((), (), s32[]{:S(2)}) async-start(), calls=%async_computation.32 | async-start | bytes 6684672 | tf_op jit(solution)/shard_map/reduce_scatter | solution.py:229
  766.7 4.3 copy-start.58
  775.7 44.4 %copy-start.52 = (f32[1024]{0:T(1024)S(1)}, f32[1024]{0:T(1024)}, u32[]{:S(2)}) copy-start(f32[1024]{0:T(1024)} %get-tuple-element.31) | copy-start | bytes 12292
  775.7 44.4 %copy-start.28 = (bf16[2,160,1024]{2,1,0:T(8,128)(2,1)S(1)}, bf16[2,160,1024]{2,1,0:T(8,128)(2,1)}, u32[]{:S(2)}) copy-start(bf16[2,160,1024]{2,1,0:T(8,128)(2,1)} %get-tuple-element.59) | copy-start | bytes 1966084
  775.7 46.7 %copy-start.2 = (bf16[4,160,1024]{2,1,0:T(8,128)(2,1)S(1)}, bf16[4,160,1024]{2,1,0:T(8,128)(2,1)}, u32[]{:S(2)}) copy-start(bf16[4,160,1024]{2,1,0:T(8,128)(2,1)} %param.9) | copy-start | bytes 3932164
  775.8 46.7 %copy-start.42 = (f32[1024]{0:T(1024)S(1)}, f32[1024]{0:T(1024)}, u32[]{:S(2)}) copy-start(f32[1024]{0:T(1024)} %copy-done.41) | copy-start | bytes 12292
  775.8 46.7 %copy-start.44 = (f32[2,160]{1,0:T(2,128)S(1)}, f32[2,160]{1,0:T(2,128)}, u32[]{:S(2)}) copy-start(f32[2,160]{1,0:T(2,128)} %copy-done.43) | copy-start | bytes 3844
  775.8 46.7 %copy-start.46 = (f32[2,160]{1,0:T(2,128)S(1)}, f32[2,160]{1,0:T(2,128)}, u32[]{:S(2)}) copy-start(f32[2,160]{1,0:T(2,128)} %copy-done.45) | copy-start | bytes 3844
  775.8 46.7 %copy-start.49 = (f32[2,160]{1,0:T(2,128)S(1)}, f32[2,160]{1,0:T(2,128)}, u32[]{:S(2)}) copy-start(f32[2,160]{1,0:T(2,128)} %copy-done.48) | copy-start | bytes 3844
  775.8 46.7 %copy-start.51 = (f32[2,160]{1,0:T(2,128)S(1)}, f32[2,160]{1,0:T(2,128)}, u32[]{:S(2)}) copy-start(f32[2,160]{1,0:T(2,128)} %copy-done.50) | copy-start | bytes 3844
  775.8 88.0 %copy-start.15 = (f32[2,160,1024]{2,1,0:T(8,128)S(1)}, f32[2,160,1024]{2,1,0:T(8,128)}, u32[]{:S(2)}) copy-start(f32[2,160,1024]{2,1,0:T(8,128)} %get-tuple-element.45) | copy-start | bytes 3932164
  (26 other events, 62.8 us)
Sparse Core Ops, SparseCore 0:
  52.2 21.4 all-gather.12
  76.0 45.2 all-gather.14
  123.4 36.7 all-gather.16
  161.6 23.1 all-gather.24
  187.4 37.5 reduce-scatter.12
  227.2 37.5 reduce-scatter.16
  267.0 50.5 all-gather.20
  319.7 22.7 all-gather.18
  344.7 50.5 all-gather.22
  396.7 22.7 all-gather.26
  421.7 38.1 reduce-scatter.14
  462.0 38.3 reduce-scatter.18
  504.2 24.2 all-gather.28
  529.9 24.2 all-gather.32
  556.3 37.5 reduce-scatter.20
  596.1 37.5 reduce-scatter.24
  640.6 24.2 all-gather.34
  666.3 24.2 all-gather.30
  702.2 37.4 reduce-scatter.26
  741.9 37.5 reduce-scatter.22
  783.8 62.3 reduce-scatter.30
  851.4 103.5 reduce-scatter.32
  960.1 104.3 reduce-scatter.34
  1069.4 84.9 reduce-scatter.28
where the time goes:
time: 1170 us; the launch traced here: 1160 us
  waiting for transfers between devices  714 us (61%)
  matrix products  166 us (14%)
  blocking collectives  152 us (13%)
  other arithmetic  74.9 us (6%)
  local copies, waits for them, and re-layouts  30.3 us (3%)
  between operations  22.1 us (2%)
    reduce_scatter x1, waiting for transfers between devices, per_device(): lax.psum_scatter(summed[5], 'dp', scatter_dimension=0, tiled=True)  110 us
    reduce_scatter x1, waiting for transfers between devices, per_device(): lax.psum_scatter(summed[2], 'dp', scatter_dimension=0, tiled=True)  89.9 us
    reduce_scatter x1, waiting for transfers between devices, per_device(): lax.psum_scatter(summed[4], 'dp', scatter_dimension=0, tiled=True)  86.4 us
    all_gather x4, waiting for transfers between devices, full_rows(): return lax.all_gather(piece, 'mp', axis=1, tiled=True)  81 us
    reduce_scatter x4, waiting for transfers between devices, row_sums(): return lax.psum_scatter(partial_rows, 'mp', scatter_dimension=1, tiled=True)  76.2 us
    unnamed x2, blocking collectives  67.8 us
    reduce_scatter x4, waiting for transfers between devices, sum_grads(): return lax.psum_scatter(partial_rows, 'mp', scatter_dimension=1, tiled=True)  63.3 us
    all_gather x4, waiting for transfers between devices, full_grads(): return lax.all_gather(piece, 'mp', axis=1, tiled=True)  53.2 us
  transfers between devices with their start and end apart: 24, of which 19 were waited for; matrix products, arithmetic and copies ran while one was open for 20% of the time, Pallas kernels for 0%

commit v1 on v0

--- a/solution.py
+++ b/solution.py
@@ -1,3 +1,4 @@
+import functools
 import jax
 import jax.numpy as jnp
 from jax import lax
@@ -6,6 +7,15 @@
 HDIM = 64
 MICRO = 2
 norm_epsilon = 1e-06
+
+
+def list_forms(payload, mesh_dim, axis_name):
+    for m in (mesh_dim, axis_name):
+        payload = lax.psum(payload, m)
+    return payload
+
+
+expand_pages_all = functools.partial(list_forms, mesh_dim="mp", axis_name="dp")
 
 
 def normalize(values):
@@ -113,7 +123,7 @@
     half_len = inputs.shape[1]
     offset = lax.axis_index("mp") * half_len
     keep_local = lax.dynamic_slice_in_dim(keep_mask, offset, half_len, 1)
-    valid_total = lax.psum(jnp.sum(keep_local).astype(jnp.float32), ("dp", "mp"))
+    valid_total = expand_pages_all(jnp.sum(keep_local).astype(jnp.float32))
     token_total = inputs.shape[0] * lax.axis_size("dp") * half_len * lax.axis_size("mp")
     loss_factor = 2.0 * token_total / valid_total
     per_micro = inputs.shape[0] // MICRO

time: 1170 us -> 1170 us (level)
    psum x1 -> x2, blocking collectives: 39.7 us -> 38.5 us  [list_forms(): payload = lax.psum(payload, m)]
where the time goes in v1:
time: 1170 us; the launch traced here: 1160 us
  waiting for transfers between devices  715 us (61%)
  matrix products  165 us (14%)
  blocking collectives  151 us (13%)
  other arithmetic  74.9 us (6%)
  local copies, waits for them, and re-layouts  30.4 us (3%)
  between operations  22.1 us (2%)
    reduce_scatter x1, waiting for transfers between devices, per_device(): lax.psum_scatter(summed[5], 'dp', scatter_dimension=0, tiled=True)  110 us
    reduce_scatter x1, waiting for transfers between devices, per_device(): lax.psum_scatter(summed[2], 'dp', scatter_dimension=0, tiled=True)  89.9 us
    reduce_scatter x1, waiting for transfers between devices, per_device(): lax.psum_scatter(summed[4], 'dp', scatter_dimension=0, tiled=True)  86.6 us
    all_gather x4, waiting for transfers between devices, full_rows(): return lax.all_gather(piece, 'mp', axis=1, tiled=True)  81 us
    reduce_scatter x4, waiting for transfers between devices, row_sums(): return lax.psum_scatter(partial_rows, 'mp', scatter_dimension=1, tiled=True)  76.2 us
    unnamed x2, blocking collectives  67.8 us
    reduce_scatter x4, waiting for transfers between devices, sum_grads(): return lax.psum_scatter(partial_rows, 'mp', scatter_dimension=1, tiled=True)  63.3 us
    all_gather x4, waiting for transfers between devices, full_grads(): return lax.all_gather(piece, 'mp', axis=1, tiled=True)  53.1 us
  transfers between devices with their start and end apart: 24, of which 19 were waited for; matrix products, arithmetic and copies ran while one was open for 20% of the time, Pallas kernels for 0%

profile of v1, /device:TPU:0, one launch (start us, length us, event | category | flops | bytes accessed | tf_op | source)
XLA Modules:
  0.0 1161.6 jit_solution(548551790545562822)
XLA Ops:
  10.9 34.9 %all-reduce.6 = (bf16[1024]{0:T(1024)(128)(2,1)S(1)}, bf16[1024]{0:T(1024)(128)(2,1)S(1)}) all-reduce(bf16[1024]{0:T(1024)(128)(2,1)S(1)} %dynamic-update-slice, bf16[1024]{0:T(1024)(128)(2,1)S(1)} %dynamic-update-slice.1), channel_id=1, replica_groups=mesh['dp'=16,'mp'=2] {'dp'}, use_global_device_ids=true, to_apply=%add | all-reduce | flops 2048 | bytes 8192
  49.3 2.8 fusion.93
  54.3 19.5 %all-gather.13.cloned.1.call-done = bf16[2,320,1024]{2,1,0:T(8,128)(2,1)} async-done(((bf16[2,160,1024]{2,1,0:T(8,128)(2,1)}), bf16[2,320,1024]{2,1,0:T(8,128)(2,1)}) %all-gather.13.cloned.1.call-update) | async-done | bytes 1310736 | tf_op jit(solution)/shard_map/all_gather | solution.py:40
  73.8 47.4 %all-gather.15.cloned.1.call-done = bf16[1024,3,512]{2,0,1:T(8,128)(2,1)} async-done(((bf16[64,3,512]{2,0,1:T(8,128)(2,1)}), bf16[1024,3,512]{2,0,1:T(8,128)(2,1)}) %all-gather.15.cloned.1.call-update) | async-done | bytes 3145744 | tf_op jit(solution)/shard_map/all_gather | solution.py:150
  121.2 4.5 fusion.54
  134.9 25.3 %all-gather.17.cloned.1.call-done = bf16[1024,512]{1,0:T(8,128)(2,1)} async-done(((bf16[64,512]{1,0:T(8,128)(2,1)}), bf16[1024,512]{1,0:T(8,128)(2,1)}) %all-gather.17.cloned.1.call-update) | async-done | bytes 1048592 | tf_op jit(solution)/shard_map/all_gather | solution.py:151
  160.2 3.9 fusion.113
  164.7 20.1 %all-gather.25.cloned.1.call-done = bf16[2,320,1024]{2,1,0:T(8,128)(2,1)} async-done(((bf16[2,160,1024]{2,1,0:T(8,128)(2,1)}), bf16[2,320,1024]{2,1,0:T(8,128)(2,1)}) %all-gather.25.cloned.1.call-update) | async-done | bytes 1310736 | tf_op jit(solution)/shard_map/all_gather | solution.py:40
  184.8 4.5 fusion.57
  198.5 2.7 fusion.111
  202.1 23.0 %reduce-scatter.13.cloned.1.call-done = f32[2,160,1024]{2,1,0:T(8,128)} async-done(((f32[2,320,1024]{2,1,0:T(8,128)}), f32[2,160,1024]{2,1,0:T(8,128)}) %reduce-scatter.13.cloned.1.call-update) | async-done | bytes 1310736 | tf_op jit(solution)/shard_map/reduce_scatter | solution.py:44
  225.1 39.8 %reduce-scatter.17.cloned.1.call-done = f32[2,160,1024]{2,1,0:T(8,128)} async-done(((f32[2,320,1024]{2,1,0:T(8,128)}), f32[2,160,1024]{2,1,0:T(8,128)}) %reduce-scatter.17.cloned.1.call-update) | async-done | bytes 1310736 | tf_op jit(solution)/shard_map/reduce_scatter | solution.py:44
  270.9 46.7 %all-gather.21.cloned.1.call-done = bf16[1024,2048]{1,0:T(8,128)(2,1)} async-done(((bf16[64,2048]{1,0:T(8,128)(2,1)}), bf16[1024,2048]{1,0:T(8,128)(2,1)}) %all-gather.21.cloned.1.call-update) | async-done | bytes 4194320 | tf_op jit(solution)/shard_map/all_gather | solution.py:152
  317.6 24.9 %all-gather.19.cloned.1.call-done = bf16[2,320,1024]{2,1,0:T(8,128)(2,1)} async-done(((bf16[2,160,1024]{2,1,0:T(8,128)(2,1)}), bf16[2,320,1024]{2,1,0:T(8,128)(2,1)}) %all-gather.19.cloned.1.call-update) | async-done | bytes 1310736 | tf_op jit(solution)/shard_map/all_gather | solution.py:40
  342.5 6.9 fusion.107
  351.7 12.9 %multiply_convert_fusion.3 = (bf16[2,320,2048]{2,1,0:T(8,128)(2,1)}, f32[2,320,2048]{2,1,0:T(8,128)}) fusion(f32[2,320,2048]{2,1,0:T(8,128)S(1)} %get-tuple-element.87, u8[320,2048]{1,0:T(8,128)(4,1)S(1)} %get-tuple-element.10, u8[320,2048]{1,0:T(8,128)(4,1)S(1)} %get-tuple-element.9), kind=kLoop, calls=%fused_computation.47 | loop fusion | flops 91750400 | bytes 14417920 | tf_op jit(solution)/shard_map/convert_element_type | solution.py:177
  364.6 30.7 %all-gather.23.cloned.1.call-done = bf16[1024,2048]{1,0:T(8,128)(2,1)} async-done(((bf16[64,2048]{1,0:T(8,128)(2,1)}), bf16[1024,2048]{1,0:T(8,128)(2,1)}) %all-gather.23.cloned.1.call-update) | async-done | bytes 4194320 | tf_op jit(solution)/shard_map/all_gather | solution.py:153
  395.3 7.4 fusion.22
  402.9 16.5 %all-gather.27.cloned.1.call-done = bf16[2,320,1024]{2,1,0:T(8,128)(2,1)} async-done(((bf16[2,160,1024]{2,1,0:T(8,128)(2,1)}), bf16[2,320,1024]{2,1,0:T(8,128)(2,1)}) %all-gather.27.cloned.1.call-update) | async-done | bytes 1310736 | tf_op jit(solution)/shard_map/all_gather | solution.py:40
  419.5 6.9 fusion.108
  426.4 12.8 %multiply_convert_fusion.2 = (bf16[2,320,2048]{2,1,0:T(8,128)(2,1)S(1)}, f32[2,320,2048]{2,1,0:T(8,128)}) fusion(f32[2,320,2048]{2,1,0:T(8,128)S(1)} %get-tuple-element.86, u8[320,2048]{1,0:T(8,128)(4,1)S(1)} %get-tuple-element.12, u8[320,2048]{1,0:T(8,128)(4,1)S(1)} %get-tuple-element.11), kind=kLoop, calls=%fused_computation.34 | loop fusion | flops 91750400 | bytes 14417920 | tf_op jit(solution)/shard_map/convert_element_type | solution.py:177
  440.7 4.4 fusion.20
  446.5 5.5 psum.36
  452.0 33.0 %psum.37 = f32[]{:T(128)} all-reduce(f32[]{:T(128)} %psum.36), channel_id=1, replica_groups=mesh['dp'=16,'mp'=2] {'dp'}, use_global_device_ids=true, to_apply=%region_23.24 | all-reduce | flops 1 | bytes 8 | tf_op jit(solution)/shard_map/psum | solution.py:14
  485.8 13.4 %reduce-scatter.19.cloned.1.call-done = f32[2,160,1024]{2,1,0:T(8,128)} async-done(((f32[2,320,1024]{2,1,0:T(8,128)}), f32[2,160,1024]{2,1,0:T(8,128)}) %reduce-scatter.19.cloned.1.call-update) | async-done | bytes 1310736 | tf_op jit(solution)/shard_map/reduce_scatter | solution.py:44
  499.2 3.6 multiply_convert_fusion.13
  503.9 23.4 %all-gather.29.cloned.1.call-done = bf16[2,320,1024]{2,1,0:T(8,128)(2,1)} async-done(((bf16[2,160,1024]{2,1,0:T(8,128)(2,1)}), bf16[2,320,1024]{2,1,0:T(8,128)(2,1)}) %all-gather.29.cloned.1.call-update) | async-done | bytes 1310736 | tf_op jit(solution)/shard_map/all_gather | solution.py:48
  527.3 10.0 add_convert_fusion.1
  538.8 4.4 fusion.26
  543.3 9.7 all-gather.33.cloned.1.call-done
  553.0 10.0 add_convert_fusion
  564.5 4.4 fusion.24
  569.1 23.5 %reduce-scatter.21.cloned.1.call-done = f32[2,160,1024]{2,1,0:T(8,128)} async-done(((f32[2,320,1024]{2,1,0:T(8,128)}), f32[2,160,1024]{2,1,0:T(8,128)}) %reduce-scatter.21.cloned.1.call-update) | async-done | bytes 1310736 | tf_op jit(solution)/shard_map/reduce_scatter | solution.py:52
  592.7 39.8 %reduce-scatter.25.cloned.1.call-done = f32[2,160,1024]{2,1,0:T(8,128)} async-done(((f32[2,320,1024]{2,1,0:T(8,128)}), f32[2,160,1024]{2,1,0:T(8,128)}) %reduce-scatter.25.cloned.1.call-update) | async-done | bytes 1310736 | tf_op jit(solution)/shard_map/reduce_scatter | solution.py:52
  632.5 4.4 multiply_reduce_fusion.2
  639.4 4.2 fusion.127
  643.6 20.1 %all-gather.35.cloned.1.call-done = bf16[2,320,1024]{2,1,0:T(8,128)(2,1)} async-done(((bf16[2,160,1024]{2,1,0:T(8,128)(2,1)}), bf16[2,320,1024]{2,1,0:T(8,128)(2,1)}) %all-gather.35.cloned.1.call-update) | async-done | bytes 1310736 | tf_op jit(solution)/shard_map/all_gather | solution.py:48
  663.7 3.0 convolution_convert_fusion
  668.9 7.2 multiply_reduce_fusion
  676.2 3.7 multiply_convert_fusion
  679.9 2.9 fusion.83
  685.0 3.8 multiply_convert_fusion.5
  691.1 3.4 multiply_convert_fusion.4
  694.9 6.1 fusion.63
  703.9 5.4 fusion.80
  710.4 5.2 multiply_reduce_fusion.1
  715.6 4.7 multiply_convert_fusion.1
  724.1 3.5 multiply_convert_fusion.6
  727.9 6.3 fusion.60
  734.3 2.5 fusion.136
  739.7 5.8 fusion.137
  745.5 6.0 bitcast_add_fusion.1
  753.2 5.0 fusion.138
  758.2 5.9 bitcast_add_fusion
  765.4 4.2 fusion.102
  769.7 4.8 bitcast_add_fusion.2
  778.3 39.3 %psum.35 = f32[]{:T(128)} all-reduce(f32[]{:T(128)S(6)} %add.143), channel_id=1, replica_groups=mesh['dp'=16,'mp'=2] {'dp','mp'}, use_global_device_ids=true, to_apply=%region_20.21 | all-reduce | flops 1 | bytes 8 | tf_op jit(solution)/shard_map/psum | solution.py:245
  821.2 2.9 fusion.98
  824.1 32.9 %all-reduce.4 = (f32[1024]{0:T(1024)S(1)}, f32[1024]{0:T(1024)S(1)}) all-reduce(f32[1024]{0:T(1024)S(1)} %add.150, f32[1024]{0:T(1024)S(1)} %add.153), channel_id=10, replica_groups=mesh['dp'=16,'mp'=2] {'dp'}, use_global_device_ids=true, to_apply=%region_40.41.clone | all-reduce | flops 2048 | bytes 16384
  857.1 5.4 all-reduce.5
  862.6 3.0 fusion.97
  867.3 86.6 %reduce-scatter.33.cloned.1.call-done = f32[64,2048]{1,0:T(8,128)} async-done(((f32[1024,2048]{1,0:T(8,128)}), f32[64,2048]{1,0:T(8,128)}) %reduce-scatter.33.cloned.1.call-update) | async-done | bytes 524304 | tf_op jit(solution)/shard_map/reduce_scatter | solution.py:241
  953.9 109.6 %reduce-scatter.35.cloned.1.call-done = f32[64,2048]{1,0:T(8,128)} async-done(((f32[1024,2048]{1,0:T(8,128)}), f32[64,2048]{1,0:T(8,128)}) %reduce-scatter.35.cloned.1.call-update) | async-done | bytes 524304 | tf_op jit(solution)/shard_map/reduce_scatter | solution.py:242
  1063.5 89.9 %reduce-scatter.29.cloned.1.call-done = f32[64,3,512]{2,0,1:T(8,128)} async-done(((f32[1024,3,512]{2,0,1:T(8,128)}), f32[64,3,512]{2,0,1:T(8,128)}) %reduce-scatter.29.cloned.1.call-update) | async-done | bytes 393232 | tf_op jit(solution)/shard_map/reduce_scatter | solution.py:239
  (253 shorter events, 72.7 us)
Async XLA Ops:
  7.2 47.1 %copy-start.47 = (s32[4,320]{1,0:T(4,128)S(1)}, s32[4,320]{1,0:T(4,128)}, u32[]{:S(2)}) copy-start(s32[4,320]{1,0:T(4,128)} %param.11) | copy-start | bytes 15364
  7.2 66.6 %all-gather.13.cloned.1.call-start = ((), (), s32[]{:S(2)}) async-start(), calls=%async_computation.12 | async-start | bytes 1966080 | tf_op jit(solution)/shard_map/all_gather | solution.py:40
  47.4 4.7 copy-start.43
  47.4 4.7 copy-start.45
  52.1 69.1 %all-gather.15.cloned.1.call-start = ((), (), s32[]{:S(2)}) async-start(), calls=%async_computation.13 | async-start | bytes 3342336 | tf_op jit(solution)/shard_map/all_gather | solution.py:150
  52.9 107.3 %all-gather.17.cloned.1.call-start = ((), (), s32[]{:S(2)}) async-start(), calls=%async_computation.14 | async-start | bytes 1114112 | tf_op jit(solution)/shard_map/all_gather | solution.py:151
  53.6 131.2 %all-gather.25.cloned.1.call-start = ((), (), s32[]{:S(2)}) async-start(), calls=%async_computation.20 | async-start | bytes 1966080 | tf_op jit(solution)/shard_map/all_gather | solution.py:40
  54.2 170.9 %reduce-scatter.13.cloned.1.call-start = ((), (), s32[]{:S(2)}) async-start(), calls=%async_computation.15 | async-start | bytes 3932160 | tf_op jit(solution)/shard_map/reduce_scatter | solution.py:44
  127.1 4.1 copy-start.18
  134.9 54.4 %copy-start.30 = (bf16[2,8,64,320]{3,2,1,0:T(8,128)(2,1)}, bf16[2,8,64,320]{3,2,1,0:T(8,128)(2,1)S(1)}, u32[]{:S(2)}) copy-start(bf16[2,8,64,320]{3,2,1,0:T(8,128)(2,1)S(1)} %fusion.79) | copy-start | bytes 1966084
  164.1 100.8 %reduce-scatter.17.cloned.1.call-start = ((), (), s32[]{:S(2)}) async-start(), calls=%async_computation.21 | async-start | bytes 3932160 | tf_op jit(solution)/shard_map/reduce_scatter | solution.py:44
  198.5 26.5 %copy-start.23 = (bf16[2,8,64,320]{3,2,1,0:T(8,128)(2,1)}, bf16[2,8,64,320]{3,2,1,0:T(8,128)(2,1)S(1)}, u32[]{:S(2)}) copy-start(bf16[2,8,64,320]{3,2,1,0:T(8,128)(2,1)S(1)} %fusion.78) | copy-start | bytes 1966084
  201.2 116.4 %all-gather.21.cloned.1.call-start = ((), (), s32[]{:S(2)}) async-start(), calls=%async_computation.17 | async-start | bytes 4456448 | tf_op jit(solution)/shard_map/all_gather | solution.py:152
  202.0 140.5 %all-gather.19.cloned.1.call-start = ((), (), s32[]{:S(2)}) async-start(), calls=%async_computation.16 | async-start | bytes 1966080 | tf_op jit(solution)/shard_map/all_gather | solution.py:40
  269.4 125.9 %all-gather.23.cloned.1.call-start = ((), (), s32[]{:S(2)}) async-start(), calls=%async_computation.18 | async-start | bytes 4456448 | tf_op jit(solution)/shard_map/all_gather | solution.py:153
  270.1 149.3 %all-gather.27.cloned.1.call-start = ((), (), s32[]{:S(2)}) async-start(), calls=%async_computation.22 | async-start | bytes 1966080 | tf_op jit(solution)/shard_map/all_gather | solution.py:40
  270.7 215.1 %reduce-scatter.15.cloned.1.call-start = ((), (), s32[]{:S(2)}) async-start(), calls=%async_computation.19 | async-start | bytes 3932160 | tf_op jit(solution)/shard_map/reduce_scatter | solution.py:44
  402.7 96.5 %reduce-scatter.19.cloned.1.call-start = ((), (), s32[]{:S(2)}) async-start(), calls=%async_computation.23 | async-start | bytes 3932160 | tf_op jit(solution)/shard_map/reduce_scatter | solution.py:44
  426.4 12.8 %copy-start.13 = (f32[2,320,2048]{2,1,0:T(8,128)}, f32[2,320,2048]{2,1,0:T(8,128)S(1)}, u32[]{:S(2)}) copy-start(f32[2,320,2048]{2,1,0:T(8,128)S(1)} %get-tuple-element.86) | copy-start | bytes 15728644
  426.4 14.3 %copy-start.57 = (bf16[1024,2048]{1,0:T(8,128)(2,1)S(1)}, bf16[1024,2048]{1,0:T(8,128)(2,1)}, u32[]{:S(2)}) copy-start(bf16[1024,2048]{1,0:T(8,128)(2,1)} %all-gather.23.cloned.1.call-done) | copy-start | bytes 12582916
  445.1 82.2 %all-gather.29.cloned.1.call-start = ((), (), s32[]{:S(2)}) async-start(), calls=%async_computation.24 | async-start | bytes 1966080 | tf_op jit(solution)/shard_map/all_gather | solution.py:48
  502.9 50.1 %all-gather.33.cloned.1.call-start = ((), (), s32[]{:S(2)}) async-start(), calls=%async_computation.28 | async-start | bytes 1966080 | tf_op jit(solution)/shard_map/all_gather | solution.py:48
  503.4 89.2 %reduce-scatter.21.cloned.1.call-start = ((), (), s32[]{:S(2)}) async-start(), calls=%async_computation.25 | async-start | bytes 3932160 | tf_op jit(solution)/shard_map/reduce_scatter | solution.py:52
  527.3 11.5 copy-start.55
  543.2 89.2 %reduce-scatter.25.cloned.1.call-start = ((), (), s32[]{:S(2)}) async-start(), calls=%async_computation.29 | async-start | bytes 3932160 | tf_op jit(solution)/shard_map/reduce_scatter | solution.py:52
  553.0 11.5 copy-start.56
  568.9 94.8 %all-gather.35.cloned.1.call-start = ((), (), s32[]{:S(2)}) async-start(), calls=%async_computation.30 | async-start | bytes 1966080 | tf_op jit(solution)/shard_map/all_gather | solution.py:48
  632.5 4.4 copy-start.4
  632.5 4.4 copy-start.5
  632.5 4.4 copy-start.14
  639.3 62.0 %all-gather.31.cloned.1.call-start = ((), (), s32[]{:S(2)}) async-start(), calls=%async_computation.26 | async-start | bytes 1966080 | tf_op jit(solution)/shard_map/all_gather | solution.py:48
  639.4 24.3 %copy-start.17 = (bf16[1024,512]{1,0:T(8,128)(2,1)S(1)}, bf16[1024,512]{1,0:T(8,128)(2,1)}, u32[]{:S(2)}) copy-start(bf16[1024,512]{1,0:T(8,128)(2,1)} %all-gather.17.cloned.1.call-done) | copy-start | bytes 3145732
  643.6 25.4 %copy-start.21 = (bf16[2,320,1,512]{1,3,0,2:T(8,128)(2,1)S(1)}, bf16[2,320,1,512]{1,3,0,2:T(8,128)(2,1)}, u32[]{:S(2)}) copy-start(bf16[2,320,1,512]{1,3,0,2:T(8,128)(2,1)} %copy-done.20) | copy-start | bytes 1966084
  643.6 177.6 %reduce-scatter.27.cloned.1.call-start = ((), (), s32[]{:S(2)}) async-start(), calls=%async_computation.31 | async-start | bytes 3932160 | tf_op jit(solution)/shard_map/reduce_scatter | solution.py:52
  668.9 7.2 slice-start
  668.9 7.2 slice-start.1
  679.9 5.2 copy-start.11
  694.8 6.4 copy-start.38
  694.9 6.4 copy-start.40
  701.0 120.2 %reduce-scatter.23.cloned.1.call-start = ((), (), s32[]{:S(2)}) async-start(), calls=%async_computation.27 | async-start | bytes 3932160 | tf_op jit(solution)/shard_map/reduce_scatter | solution.py:52
  703.9 6.5 copy-start.19
  715.6 6.6 copy-start.9
  727.9 6.3 copy-start.36
  727.9 6.4 copy-start.31
  734.3 133.0 %reduce-scatter.31.cloned.1.call-start = ((), (), s32[]{:S(2)}) async-start(), calls=%async_computation.33 | async-start | bytes 2228224 | tf_op jit(solution)/shard_map/reduce_scatter | solution.py:240
  739.2 6.3 copy-start.59
  739.2 214.7 %reduce-scatter.33.cloned.1.call-start = ((), (), s32[]{:S(2)}) async-start(), calls=%async_computation.34 | async-start | bytes 8912896 | tf_op jit(solution)/shard_map/reduce_scatter | solution.py:241
  739.7 5.8 copy-start.62
  751.5 312.0 %reduce-scatter.35.cloned.1.call-start = ((), (), s32[]{:S(2)}) async-start(), calls=%async_computation.35 | async-start | bytes 8912896 | tf_op jit(solution)/shard_map/reduce_scatter | solution.py:242
  753.2 5.0 copy-start.27
  753.2 5.0 copy-start.60
  764.1 5.5 copy-start.32
  764.1 5.5 copy-start.33
  764.1 389.3 %reduce-scatter.29.cloned.1.call-start = ((), (), s32[]{:S(2)}) async-start(), calls=%async_computation.32 | async-start | bytes 6684672 | tf_op jit(solution)/shard_map/reduce_scatter | solution.py:239
  765.4 4.3 copy-start.58
  774.5 44.4 %copy-start.52 = (f32[1024]{0:T(1024)S(1)}, f32[1024]{0:T(1024)}, u32[]{:S(2)}) copy-start(f32[1024]{0:T(1024)} %get-tuple-element.31) | copy-start | bytes 12292
  774.5 44.5 %copy-start.28 = (bf16[2,160,1024]{2,1,0:T(8,128)(2,1)S(1)}, bf16[2,160,1024]{2,1,0:T(8,128)(2,1)}, u32[]{:S(2)}) copy-start(bf16[2,160,1024]{2,1,0:T(8,128)(2,1)} %get-tuple-element.59) | copy-start | bytes 1966084
  774.5 46.7 %copy-start.2 = (bf16[4,160,1024]{2,1,0:T(8,128)(2,1)S(1)}, bf16[4,160,1024]{2,1,0:T(8,128)(2,1)}, u32[]{:S(2)}) copy-start(bf16[4,160,1024]{2,1,0:T(8,128)(2,1)} %param.9) | copy-start | bytes 3932164
  774.5 46.7 %copy-start.42 = (f32[1024]{0:T(1024)S(1)}, f32[1024]{0:T(1024)}, u32[]{:S(2)}) copy-start(f32[1024]{0:T(1024)} %copy-done.41) | copy-start | bytes 12292
  774.5 46.7 %copy-start.44 = (f32[2,160]{1,0:T(2,128)S(1)}, f32[2,160]{1,0:T(2,128)}, u32[]{:S(2)}) copy-start(f32[2,160]{1,0:T(2,128)} %copy-done.43) | copy-start | bytes 3844
  774.5 46.7 %copy-start.46 = (f32[2,160]{1,0:T(2,128)S(1)}, f32[2,160]{1,0:T(2,128)}, u32[]{:S(2)}) copy-start(f32[2,160]{1,0:T(2,128)} %copy-done.45) | copy-start | bytes 3844
  774.5 46.7 %copy-start.49 = (f32[2,160]{1,0:T(2,128)S(1)}, f32[2,160]{1,0:T(2,128)}, u32[]{:S(2)}) copy-start(f32[2,160]{1,0:T(2,128)} %copy-done.48) | copy-start | bytes 3844
  774.5 46.7 %copy-start.51 = (f32[2,160]{1,0:T(2,128)S(1)}, f32[2,160]{1,0:T(2,128)}, u32[]{:S(2)}) copy-start(f32[2,160]{1,0:T(2,128)} %copy-done.50) | copy-start | bytes 3844
  774.6 88.0 %copy-start.15 = (f32[2,160,1024]{2,1,0:T(8,128)S(1)}, f32[2,160,1024]{2,1,0:T(8,128)}, u32[]{:S(2)}) copy-start(f32[2,160,1024]{2,1,0:T(8,128)} %get-tuple-element.45) | copy-start | bytes 3932164
  (26 other events, 62.8 us)
Sparse Core Ops, SparseCore 0:
  52.2 21.4 all-gather.12
  76.0 45.2 all-gather.14
  123.4 36.7 all-gather.16
  161.6 23.1 all-gather.24
  187.4 37.5 reduce-scatter.12
  227.2 37.5 reduce-scatter.16
  267.0 50.5 all-gather.20
  319.7 22.7 all-gather.18
  344.7 50.5 all-gather.22
  396.7 22.7 all-gather.26
  421.7 37.6 reduce-scatter.14
  461.6 37.5 reduce-scatter.18
  503.0 24.2 all-gather.28
  528.7 24.2 all-gather.32
  555.1 37.5 reduce-scatter.20
  594.9 37.5 reduce-scatter.24
  639.4 24.2 all-gather.34
  665.1 24.2 all-gather.30
  701.1 37.4 reduce-scatter.26
  740.8 37.5 reduce-scatter.22
  782.8 62.1 reduce-scatter.30
  850.2 103.6 reduce-scatter.32
  959.1 104.4 reduce-scatter.34
  1068.4 84.9 reduce-scatter.28
